TPU v7x, 1024 devices: a whole 4x8x16 slice. The times are simulated.
1024 devices in a mesh: section: 2 (over core), ctx: 32 (over y, x), tp: 16 (over z).
Axes of the slice: x: 4, y: 8, z: 16, core: 2. Of those that a mesh axis runs over, the one named last changes fastest.
Arguments:
- activations: bfloat16 [2, 4096, 4096], P(None, 'ctx', 'tp'), may hold values from -6 to 6
- norm_gain: float32 [2, 4096], P('section'), may hold values from 0.1 to 1.9
- value_projection: bfloat16 [2, 4096, 4096], P('section', None, 'tp'), may hold values from -0.09375 to 0.09375
- short_taps: float32 [2, 3, 3, 4096], P('section', None, None, 'tp'), may hold values from -3 to 3
- long_taps: bfloat16 [2, 256, 128], P('section', 'tp'), may hold values from -0.5 to 0.5
- skip_gain: float32 [2, 4096], P('section', 'tp'), may hold values from -4 to 4
- out_projection: bfloat16 [2, 4096, 4096], P('section', 'tp'), may hold values from -0.09375 to 0.09375
Outputs:
- layer_out: bfloat16 [2, 4096, 4096], P('section', 'ctx', 'tp')
All inputs are finite; a program needn't handle non-finite values.
Results may differ from a plain program's by a relative error of at most 0.012.
The roundings to bfloat16 on the way count: a program that leaves them out, or rounds other values in their place, can miss the bound.
Values may be sent and summed in bfloat16 or wider, within the bound.
A program may use at most 32 MiB of HBM per device.

v0:
```python
import jax
import jax.numpy as jnp
from jax import lax
from jax.sharding import PartitionSpec as P

EPS = 1e-06


def from_behind(shard, axis, by):
    count = lax.axis_size(axis)
    pairs = [(i, i + by) for i in range(count) if 0 <= i + by < count]
    return lax.ppermute(shard, axis, pairs)


def swapped(array):
    return lax.ppermute(array, "section", [(0, 1), (1, 0)])


def toeplitz(taps, rows):
    groups, filt = taps.shape
    period = 2 * filt
    v = jnp.concatenate([jnp.flip(taps, axis=1), jnp.zeros_like(taps)], axis=1)
    tiled = jnp.tile(v, (1, rows))[:, : rows * (period - 1)]
    return tiled.reshape(groups * rows, period - 1)


def layer(current, gain, flat, short, taps, skip, out_weight):
    rows, local = current.shape
    width = flat.shape[0]
    group_count, filt = taps.shape
    group_width = local // group_count
    column = lax.axis_index("tp") * local
    local_gain = lax.dynamic_slice_in_dim(gain, column, local)
    matrix = toeplitz(taps, rows)
    whole = lax.all_gather(current, "tp", axis=1, tiled=True)
    whole_f = whole.astype(jnp.float32)
    squares = jnp.sum(whole_f * whole_f, axis=1, keepdims=True)
    normed = (whole_f * gain).astype(jnp.bfloat16)
    raw_proj = jnp.dot(normed, flat, preferred_element_type=jnp.float32)
    scale = lax.rsqrt(squares / width + EPS)
    values = (raw_proj * scale).astype(jnp.bfloat16)
    own = current.astype(jnp.float32)
    own_normed = lax.optimization_barrier((own * local_gain).astype(jnp.bfloat16))
    query = (own_normed.astype(jnp.float32) * scale).astype(jnp.bfloat16)
    both = jnp.stack([query, values], axis=0)
    rim = from_behind(both[:, rows - 2 :], "ctx", 1)
    padded = jnp.concatenate([rim, both], axis=1).astype(jnp.float32)

    def featured(index, source):
        p = padded[source]
        return short[0, index] * p[2:] + short[1, index] * p[1:-1] + short[2, index] * p[:-2]

    product = (featured(1, 0) * featured(2, 1)).astype(jnp.bfloat16)
    before = from_behind(product[rows - (filt - 1) :], "ctx", 1)
    extended = jnp.concatenate([before, product], axis=0)
    all_groups = jnp.dot(matrix, extended, preferred_element_type=jnp.float32)
    all_groups = all_groups.reshape(group_count, rows, local)
    group_of = lax.broadcasted_iota(jnp.int32, all_groups.shape, 2) // group_width
    mine = lax.broadcasted_iota(jnp.int32, all_groups.shape, 0) == group_of
    filtered = jnp.sum(jnp.where(mine, all_groups, 0.0), axis=0)
    mixed = filtered + skip * product.astype(jnp.float32)
    gated = (featured(0, 0) * mixed).astype(jnp.bfloat16)
    terms = jnp.dot(gated, out_weight, preferred_element_type=jnp.float32).astype(jnp.bfloat16)
    summed = lax.psum_scatter(terms, "tp", scatter_dimension=1, tiled=True)
    return (own + summed.astype(jnp.float32)).astype(jnp.bfloat16)


def body(
    activations, norm_gain, value_projection, short_taps, long_taps, skip_gain, out_projection
):
    section = lax.axis_index("section")
    first = section == 0
    own = (
        norm_gain[0],
        value_projection[0],
        short_taps[0],
        long_taps[0],
        skip_gain[0],
        out_projection[0],
    )
    other = [swapped(a) for a in own]
    current = lax.dynamic_index_in_dim(activations, section, 0, keepdims=False)
    current = layer(current, *[jnp.where(first, a, b) for a, b in zip(own, other)])
    current = layer(current, *[jnp.where(first, b, a) for a, b in zip(own, other)])
    return current[None]


def solution(mesh):
    in_specs = (
        P(None, "ctx", "tp"),
        P("section", None),
        P("section", None, "tp"),
        P("section", None, None, "tp"),
        P("section", "tp", None),
        P("section", "tp"),
        P("section", "tp", None),
    )
    out_specs = P("section", "ctx", "tp")
    return jax.shard_map(body, mesh=mesh, in_specs=in_specs, out_specs=out_specs, check_vma=False)
```

profile of v0, /device:TPU:6, one launch (start us, length us, event | category | flops | bytes accessed | tf_op | source)
XLA Modules:
  0.0 371.1 jit_solution(934697636014076078)
XLA Ops:
  6.5 1.9 collective-permute-start.1
  8.5 1.4 collective-permute-done.1
  9.8 0.7 broadcast_select_fusion.1
  10.6 1.5 fusion.39
  12.2 2.1 collective-permute-start.2
  14.9 2.2 collective-permute-start
  17.2 2.1 collective-permute-start.4
  19.3 2.3 collective-permute-start.6
  21.5 2.1 collective-permute-start.7
  24.7 1.3 broadcast_select_fusion.6
  26.7 69.6 %all-gather.6.cloned.1.call-done = bf16[1,128,4096]{2,1,0:T(8,128)(2,1)} async-done(((bf16[1,128,256]{2,1,0:T(8,128)(2,1)}), bf16[1,128,4096]{2,1,0:T(8,128)(2,1)}) %all-gather.6.cloned.1.call-update) | async-done | bytes 1048592 | tf_op jit(solution)/shard_map/all_gather | solution.py:35
  96.3 1.5 fusion.2
  97.9 3.2 fusion.26
  101.2 3.4 collective-permute-start.3
  105.2 1.5 collective-permute-done.3
  106.8 5.5 %collective-permute-start.5 = (bf16[127,256]{1,0:T(8,128)(2,1)S(1)}, bf16[127,256]{1,0:T(8,128)(2,1)S(1)}, u32[]{:S(2)}, u32[]{:S(2)}) collective-permute-start(bf16[127,256]{1,0:T(8,128)(2,1)S(1)} %slice.232), channel_id=1, source_target_pairs={{0,16},{16,32},{32,48},{48,64},{64,80},{80,96},{96,112},{112,128},... | collective-permute-start | bytes 195080 | tf_op jit(solution)/shard_map/ppermute | solution.py:12
  113.2 3.4 dot_general.23
  117.2 1.5 select_reduce_fusion.1
  118.9 1.6 convolution_convert_fusion.1
  120.6 70.5 %reduce-scatter.3.cloned.1.call-done = bf16[128,256]{1,0:T(8,128)(2,1)} async-done(((bf16[128,4096]{1,0:T(8,128)(2,1)}), bf16[128,256]{1,0:T(8,128)(2,1)}) %reduce-scatter.3.cloned.1.call-update) | async-done | bytes 65552 | tf_op jit(solution)/shard_map/reduce_scatter | solution.py:64
  191.1 1.5 fusion.37
  192.7 74.4 %all-gather.4.cloned.1.call-done = bf16[128,4096]{1,0:T(8,128)(2,1)} async-done(((bf16[128,256]{1,0:T(8,128)(2,1)}), bf16[128,4096]{1,0:T(8,128)(2,1)}) %all-gather.4.cloned.1.call-update) | async-done | bytes 1048592 | tf_op jit(solution)/shard_map/all_gather | solution.py:35
  267.0 1.5 fusion
  268.7 3.0 fusion.29
  271.7 3.4 collective-permute-start.8
  275.1 2.1 collective-permute-done.8
  277.4 5.5 %collective-permute-start.9 = (bf16[127,256]{1,0:T(8,128)(2,1)S(1)}, bf16[127,256]{1,0:T(8,128)(2,1)}, u32[]{:S(2)}, u32[]{:S(2)}) collective-permute-start(bf16[127,256]{1,0:T(8,128)(2,1)S(1)} %slice.249), channel_id=1, source_target_pairs={{0,16},{16,32},{32,48},{48,64},{64,80},{80,96},{96,112},{112,128},... | collective-permute-start | bytes 195080 | tf_op jit(solution)/shard_map/ppermute | solution.py:12
  283.7 4.4 %dot_general.27 = bf16[16,128,255]{2,1,0:T(8,128)(2,1)} reshape(bf16[16,32640]{1,0:T(8,128)(2,1)S(1)} %slice.239) | data formatting | bytes 2088960 | tf_op jit(solution)/shard_map/dot_general | solution.py:56
  288.1 1.8 select_reduce_fusion
  289.9 3.3 convolution_convert_fusion
  293.2 69.9 %reduce-scatter.5.cloned.1.call-done = bf16[128,256]{1,0:T(8,128)(2,1)} async-done(((bf16[128,4096]{1,0:T(8,128)(2,1)}), bf16[128,256]{1,0:T(8,128)(2,1)}) %reduce-scatter.5.cloned.1.call-update) | async-done | bytes 65552 | tf_op jit(solution)/shard_map/reduce_scatter | solution.py:64
  363.1 1.5 fusion.61
  (69 shorter events, 6.4 us)
Async XLA Ops:
  6.5 89.7 %all-gather.6.cloned.1.call-start = ((), (), s32[]{:S(2)}) async-start(), calls=%async_computation.5 | async-start | bytes 1114112 | tf_op jit(solution)/shard_map/all_gather | solution.py:35
  6.5 3.3 collective-permute-start.1
  12.1 179.0 %reduce-scatter.3.cloned.1.call-start = ((), (), s32[]{:S(2)}) async-start(), calls=%async_computation.2 | async-start | bytes 1114112 | tf_op jit(solution)/shard_map/reduce_scatter | solution.py:64
  12.2 85.7 %collective-permute-start.2 = (bf16[4096,256]{1,0:T(8,128)(2,1)}, bf16[4096,256]{1,0:T(8,128)(2,1)S(1)}, u32[]{:S(2)}, u32[]{:S(2)}) collective-permute-start(bf16[4096,256]{1,0:T(8,128)(2,1)} %bitcast.201), channel_id=1, source_target_pairs={{0,512},{512,0},{1,513},{513,1},{2,514},{514,2},{3,515},{515,3},{4... | collective-permute-start | bytes 6291464 | tf_op jit(solution)/shard_map/ppermute | solution.py:16
  14.9 11.0 %collective-permute-start = (f32[3,3,256]{2,1,0:T(4,128)S(1)}, f32[3,3,256]{2,1,0:T(4,128)S(1)}, u32[]{:S(2)}, u32[]{:S(2)}) collective-permute-start(f32[3,3,256]{2,1,0:T(4,128)S(1)} %bitcast.179), channel_id=1, source_target_pairs={{0,512},{512,0},{1,513},{513,1},{2,514},{514,2},{3,515},{515,3},{4... | collective-permute-start | bytes 27656 | tf_op jit(solution)/shard_map/ppermute | solution.py:16
  17.2 95.1 %collective-permute-start.4 = (bf16[16,128]{1,0:T(8,128)(2,1)}, bf16[16,128]{1,0:T(8,128)(2,1)S(1)}, u32[]{:S(2)}, u32[]{:S(2)}) collective-permute-start(bf16[16,128]{1,0:T(8,128)(2,1)} %bitcast.198), channel_id=1, source_target_pairs={{0,512},{512,0},{1,513},{513,1},{2,514},{514,2},{3,515},{515,3},{4... | collective-permute-start | bytes 12296 | tf_op jit(solution)/shard_map/ppermute | solution.py:16
  19.3 5.4 %collective-permute-start.6 = (f32[256]{0:T(256)}, f32[256]{0:T(256)S(1)}, u32[]{:S(2)}, u32[]{:S(2)}) collective-permute-start(f32[256]{0:T(256)} %bitcast.199), channel_id=1, source_target_pairs={{0,512},{512,0},{1,513},{513,1},{2,514},{514,2},{3,515},{515,3},{4... | collective-permute-start | bytes 3080 | tf_op jit(solution)/shard_map/ppermute | solution.py:16
  21.5 97.2 %collective-permute-start.7 = (bf16[256,4096]{1,0:T(8,128)(2,1)}, bf16[256,4096]{1,0:T(8,128)(2,1)}, u32[]{:S(2)}, u32[]{:S(2)}) collective-permute-start(bf16[256,4096]{1,0:T(8,128)(2,1)} %bitcast.172), channel_id=1, source_target_pairs={{0,512},{512,0},{1,513},{513,1},{2,514},{514,2},{3,515},{515,3},{4... | collective-permute-start | bytes 6291464 | tf_op jit(solution)/shard_map/ppermute | solution.py:16
  97.9 14.4 %copy-start.7 = (bf16[1,16,128]{2,1,0:T(8,128)(2,1)S(1)}, bf16[1,16,128]{2,1,0:T(8,128)(2,1)}, u32[]{:S(2)}) copy-start(bf16[1,16,128]{2,1,0:T(8,128)(2,1)} %param.11) | copy-start | bytes 12292
  97.9 3.3 copy-start.10
  101.2 5.5 %collective-permute-start.3 = (bf16[2,2,256]{2,1,0:T(2,128)(2,1)S(1)}, bf16[2,2,256]{2,1,0:T(2,128)(2,1)S(1)}, u32[]{:S(2)}, u32[]{:S(2)}) collective-permute-start(bf16[2,2,256]{2,1,0:T(2,128)(2,1)S(1)} %pad_maximum_fusion.1), channel_id=1, source_target_pairs={{0,16},{16,32},{32,48},{48,64},{64,80},{80,96},{96,112},{112,128},... | collective-permute-start | bytes 6152 | tf_op jit(solution)/shard_map/ppermute | solution.py:12
  106.8 9.8 %collective-permute-start.5 = (bf16[127,256]{1,0:T(8,128)(2,1)S(1)}, bf16[127,256]{1,0:T(8,128)(2,1)S(1)}, u32[]{:S(2)}, u32[]{:S(2)}) collective-permute-start(bf16[127,256]{1,0:T(8,128)(2,1)S(1)} %slice.232), channel_id=1, source_target_pairs={{0,16},{16,32},{32,48},{48,64},{64,80},{80,96},{96,112},{112,128},... | collective-permute-start | bytes 195080 | tf_op jit(solution)/shard_map/ppermute | solution.py:12
  113.1 4.1 %copy-start.8 = (s32[256]{0:T(256)S(1)}, s32[256]{0:T(256)}, u32[]{:S(2)}) copy-start(s32[256]{0:T(256)} %get-tuple-element.44) | copy-start | bytes 3076
  116.6 0.6 copy-start.11
  117.2 1.6 copy-start
  118.9 72.3 %copy-start.1 = (bf16[1,128,256]{2,1,0:T(8,128)(2,1)S(1)}, bf16[1,128,256]{2,1,0:T(8,128)(2,1)}, u32[]{:S(2)}) copy-start(bf16[1,128,256]{2,1,0:T(8,128)(2,1)} %get-tuple-element.8) | copy-start | bytes 196612
  120.5 146.5 %all-gather.4.cloned.1.call-start = ((), (), s32[]{:S(2)}) async-start(), calls=%async_computation.3 | async-start | bytes 1114112 | tf_op jit(solution)/shard_map/all_gather | solution.py:35
  192.6 170.5 %reduce-scatter.5.cloned.1.call-start = ((), (), s32[]{:S(2)}) async-start(), calls=%async_computation.4 | async-start | bytes 1114112 | tf_op jit(solution)/shard_map/reduce_scatter | solution.py:64
  271.7 5.5 %collective-permute-start.8 = (bf16[2,2,256]{2,1,0:T(2,128)(2,1)S(1)}, bf16[2,2,256]{2,1,0:T(2,128)(2,1)S(1)}, u32[]{:S(2)}, u32[]{:S(2)}) collective-permute-start(bf16[2,2,256]{2,1,0:T(2,128)(2,1)S(1)} %pad_maximum_fusion), channel_id=1, source_target_pairs={{0,16},{16,32},{32,48},{48,64},{64,80},{80,96},{96,112},{112,128},... | collective-permute-start | bytes 6152 | tf_op jit(solution)/shard_map/ppermute | solution.py:12
  277.4 10.7 %collective-permute-start.9 = (bf16[127,256]{1,0:T(8,128)(2,1)S(1)}, bf16[127,256]{1,0:T(8,128)(2,1)}, u32[]{:S(2)}, u32[]{:S(2)}) collective-permute-start(bf16[127,256]{1,0:T(8,128)(2,1)S(1)} %slice.249), channel_id=1, source_target_pairs={{0,16},{16,32},{32,48},{48,64},{64,80},{80,96},{96,112},{112,128},... | collective-permute-start | bytes 195080 | tf_op jit(solution)/shard_map/ppermute | solution.py:12
  283.6 4.5 %copy-start.9 = (s32[256]{0:T(256)S(1)}, s32[256]{0:T(256)}, u32[]{:S(2)}) copy-start(s32[256]{0:T(256)} %get-tuple-element.44) | copy-start | bytes 3076
  288.1 1.8 copy-start.3
  288.1 1.8 copy-start.4
  288.1 1.8 copy-start.5
  288.1 1.8 copy-start.6
  289.9 73.2 %copy-start.2 = (bf16[128,256]{1,0:T(8,128)(2,1)S(1)}, bf16[128,256]{1,0:T(8,128)(2,1)}, u32[]{:S(2)}) copy-start(bf16[128,256]{1,0:T(8,128)(2,1)} %get-tuple-element.6) | copy-start | bytes 196612
Sparse Core Ops, SparseCore 0:
  12.2 83.9 all-gather.5
  120.6 70.4 reduce-scatter.2
  194.0 72.9 all-gather.3
  293.3 69.7 reduce-scatter.4
where the time goes:
time: 372 us; the launch traced here: 371 us
  waiting for transfers between devices  289 us (78%)
  starting transfers between devices  30.5 us (8%)
  matrix products  14.4 us (4%)
  between operations  13.5 us (4%)
  other arithmetic  11.7 us (3%)
  local copies, waits for them, and re-layouts  11.7 us (3%)
    all_gather x2, waiting for transfers between devices, layer(): whole = lax.all_gather(current, 'tp', axis=1, tiled=True)  144 us
    reduce_scatter x2, waiting for transfers between devices, layer(): summed = lax.psum_scatter(terms, 'tp', scatter_dimension=1, tiled=True)  140 us
    ppermute x4, starting transfers between devices, from_behind(): return lax.ppermute(shard, axis, pairs)  17.7 us
    ppermute x6, starting transfers between devices, swapped(): return lax.ppermute(array, 'section', [(0, 1), (1, 0)])  12.6 us
    dot_general x2, local copies, waits for them, and re-layouts, layer(): all_groups = jnp.dot(matrix, extended, preferred_element_type=jnp.float32)  7.72 us
  transfers between devices with their start and end apart: 14, of which 7 were waited for; matrix products, arithmetic and copies ran while one was open for 5% of the time, Pallas kernels for 0%

commit v1 on v0

v1 whole, which is shorter than its diff:
```python
import jax
import jax.numpy as jnp
from jax import lax
from jax.experimental import pallas as pl
from jax.experimental.pallas import tpu as pltpu
from jax.sharding import PartitionSpec as P

EPS = 1e-06
CHUNKS = 2
TAIL = 16
MESH = pl.DeviceIdType.MESH
F32 = jnp.float32
BF16 = jnp.bfloat16


def kernel(
    ring, chain, rows, local, groups, lag,
    act, par_in, wv_in, wo_in, out,
    whole, par, wv, wo, matrix, conv, acc, ssq, qx, vx, qv, halo, tail, term, sent, got,
    act_sem, par_sem, wv_sem, wo_sem, swap_sem,
    ag_s, ag_r, halo_s, halo_r, rs_s, rs_r,
):
    s = lax.axis_index("section")
    c = lax.axis_index("ctx")
    z = lax.axis_index("tp")
    half = ring // 2
    width = ring * local
    group_width = local // groups
    part = rows // CHUNKS
    on_z = (lax.rem(z + 1, ring), lax.rem(z + ring - 1, ring))
    ahead = lax.rem(c + 1, chain)
    ahead2 = lax.rem(c + 2, chain)
    behind = lax.rem(c + chain - 1, chain)
    behind2 = lax.rem(c + chain - 2, chain)
    taps_at = TAIL
    gain_at = TAIL + groups

    barrier = pltpu.get_barrier_semaphore()
    for there in (
        {"section": 1 - s}, {"tp": on_z[0]}, {"tp": on_z[1]},
        {"ctx": ahead}, {"ctx": ahead2}, {"ctx": behind}, {"ctx": behind2},
    ):
        pl.semaphore_signal(barrier, inc=1, device_id=there, device_id_type=MESH)

    own = pltpu.make_async_copy(act.at[s], whole.at[0, z], act_sem)
    own.start()
    weights = ((wv_in, wv, wv_sem), (par_in, par, par_sem), (wo_in, wo, wo_sem))
    for source, held, sem in weights:
        pltpu.make_async_copy(source, held.at[s], sem.at[s]).start()
    pl.semaphore_wait(barrier, 7)

    def swap(index):
        source, held, sem = weights[index]
        return pltpu.make_async_remote_copy(
            source, held.at[s], swap_sem.at[index], sem.at[s],
            device_id={"section": 1 - s}, device_id_type=MESH,
        )

    def ready(layer, index):
        source, held, sem = weights[index]
        pltpu.make_async_copy(source, held.at[layer], sem.at[layer]).wait()

    def piece(q):
        return pl.ds(q * part, part)

    def origin(d, k):
        return lax.rem(z + ring - k, ring) if d == 0 else lax.rem(z + k, ring)

    def gather(layer, d, k, q, received=False):
        block = whole.at[layer, origin(d, k + 1 if received else k), piece(q)]
        return pltpu.make_async_remote_copy(
            block, block, ag_s.at[layer, d, k, q], ag_r.at[layer, d, k, q],
            device_id={"tp": on_z[d]}, device_id_type=MESH,
        )

    def scatter(layer, d, k, q):
        return pltpu.make_async_remote_copy(
            sent.at[layer, d, k, piece(q)], got.at[layer, d, k, piece(q)],
            rs_s.at[layer, d, k, q], rs_r.at[layer, d, k, q],
            device_id={"tp": on_z[d]}, device_id_type=MESH,
        )

    def halo_copy(layer):
        return pltpu.make_async_remote_copy(
            qv.at[layer], halo.at[layer], halo_s.at[layer, 0], halo_r.at[layer, 0],
            device_id={"ctx": ahead}, device_id_type=MESH,
        )

    def tail_copy(layer):
        return pltpu.make_async_remote_copy(
            qv.at[layer, :, pl.ds(rows - TAIL, TAIL)], tail.at[layer],
            halo_s.at[layer, 1], halo_r.at[layer, 1],
            device_id={"ctx": ahead2}, device_id_type=MESH,
        )

    gathers = (half, half - 1)
    scatters = (half - 1, half)

    own.wait()
    for layer in range(2):
        for q in range(CHUNKS):
            for d in range(2):
                gather(layer, d, 0, q).start()
        if layer == 0:
            for index in range(3):
                swap(index).start()
        acc[...] = jnp.zeros_like(acc)
        ssq[...] = jnp.zeros_like(ssq)

        def project(o, layer=layer):
            x = whole[layer, o].astype(F32)
            squared = x * x
            lanes = squared[:, :128]
            for at in range(128, local, 128):
                lanes = lanes + squared[:, at : at + 128]
            ssq[...] += lanes
            normed = (x * par[layer, pl.ds(gain_at + o, 1), :]).astype(BF16)
            acc[...] += jnp.dot(normed, wv[layer, o], preferred_element_type=F32)

        def build(g, layer=layer):
            row = par[layer, pl.ds(taps_at + g, 1), :]
            base = jnp.broadcast_to(row, (rows, 2 * rows))
            turned = pltpu.roll(base, 0, 1, stride=1, stride_axis=0)
            matrix[g * rows : (g + 1) * rows, :] = turned.astype(BF16)

        pending = [z]
        built = 0
        waited = False
        for k in range(half):
            for q in range(CHUNKS):
                for d in range(2):
                    if k < gathers[d]:
                        gather(layer, d, k, q, received=True).wait_recv()
                        if k + 1 < gathers[d]:
                            gather(layer, d, k + 1, q).start()
            for d in range(2):
                if k < gathers[d]:
                    pending.append(origin(d, k + 1))
            if layer == 0 and k < lag:
                continue
            if not waited:
                ready(layer, 0)
                ready(layer, 1)
                waited = True
            count = 4 if k + 1 < half else len(pending)
            for o in pending[:count]:
                project(o)
            pending = pending[count:]
            goal = groups * (k + 1) // half
            for g in range(built, goal):
                build(g)
            built = goal

        def short(i, which, layer=layer):
            return par[layer, i * 3 + which : i * 3 + which + 1, :]

        def featured(which, x, start, count):
            return (
                short(0, which) * x[start : start + count, :]
                + short(1, which) * x[start - 1 : start - 1 + count, :]
                + short(2, which) * x[start - 2 : start - 2 + count, :]
            )

        scale = lax.rsqrt(jnp.sum(ssq[...], axis=1, keepdims=True) / width + EPS)
        values = (acc[...] * scale).astype(BF16)
        normed = (whole[layer, z].astype(F32) * par[layer, pl.ds(gain_at + z, 1), :]).astype(BF16)
        query = (normed.astype(F32) * scale).astype(BF16)
        qv[layer, 1] = values
        qv[layer, 0] = query
        halo_copy(layer).start()
        tail_copy(layer).start()
        qx[TAIL + rows :, :] = query.astype(F32)
        vx[TAIL + rows :, :] = values.astype(F32)
        halo_copy(layer).wait_recv()
        tail_copy(layer).wait_recv()
        for index, x in ((0, qx), (1, vx)):
            x[TAIL : TAIL + rows, :] = jnp.where(c > 0, halo[layer, index].astype(F32), 0.0)
            x[:TAIL, :] = jnp.where(c > 1, tail[layer, index].astype(F32), 0.0)
        product = (
            featured(1, qx, TAIL, 2 * rows) * featured(2, vx, TAIL, 2 * rows)
        ).astype(BF16)
        conv[...] = jnp.dot(matrix[...], product, preferred_element_type=F32)
        group_of = lax.broadcasted_iota(jnp.int32, (rows, local), 1) // group_width
        filtered = conv[:rows, :]
        for g in range(1, groups):
            filtered = jnp.where(group_of == g, conv[g * rows : (g + 1) * rows, :], filtered)
        skip = par[layer, 9:10, :]
        mixed = filtered + skip * product[rows:, :].astype(F32)
        gated = (featured(0, qx, TAIL + rows, rows) * mixed).astype(BF16)

        if layer == 0:
            ready(0, 2)
        else:
            ready(1, 2)

        def terms(dest, layer=layer, gated=gated):
            columns = pl.ds(pl.multiple_of(dest * local, local), local)
            return jnp.dot(gated, wo[layer, :, columns], preferred_element_type=F32)

        def dest(d, k):
            if d == 0:
                return lax.rem(z + half - 1 - k, ring)
            return lax.rem(z + ring - half + k, ring)

        for d in range(2):
            sent[layer, d, 0] = terms(dest(d, 0)).astype(BF16)
            for q in range(CHUNKS):
                scatter(layer, d, 0, q).start()
        for k in range(1, half):
            for d in range(2):
                if k < scatters[d]:
                    term[d] = terms(dest(d, k))
            for q in range(CHUNKS):
                for d in range(2):
                    if k < scatters[d]:
                        scatter(layer, d, k - 1, q).wait_recv()
                        sent[layer, d, k, piece(q)] = (
                            term[d, piece(q)] + got[layer, d, k - 1, piece(q)].astype(F32)
                        ).astype(BF16)
                        scatter(layer, d, k, q).start()
        term[0] = whole[layer, z].astype(F32)
        term[1] = terms(z)
        for q in range(CHUNKS):
            for d in range(2):
                scatter(layer, d, scatters[d] - 1, q).wait_recv()
            summed = (
                term[1, piece(q)]
                + got[layer, 0, scatters[0] - 1, piece(q)].astype(F32)
                + got[layer, 1, scatters[1] - 1, piece(q)].astype(F32)
            )
            result = (term[0, piece(q)] + summed).astype(BF16)
            if layer == 0:
                whole[1, z, piece(q)] = result
            else:
                out[piece(q), :] = result

    for index in range(3):
        swap(index).wait_send()
    for layer in range(2):
        halo_copy(layer).wait_send()
        tail_copy(layer).wait_send()
        for d in range(2):
            for q in range(CHUNKS):
                for k in range(gathers[d]):
                    gather(layer, d, k, q).wait_send()
                for k in range(scatters[d]):
                    scatter(layer, d, k, q).wait_send()


def body(
    activations, norm_gain, value_projection, short_taps, long_taps, skip_gain, out_projection
):
    ring = lax.axis_size("tp")
    chain = lax.axis_size("ctx")
    rows, local = activations.shape[1:]
    width = value_projection.shape[1]
    groups, filt = long_taps.shape[1:]
    half = ring // 2
    taps = jnp.flip(long_taps[0].astype(F32), axis=1)
    par = jnp.concatenate(
        [
            short_taps[0].reshape(9, local),
            skip_gain,
            jnp.zeros((TAIL - 10, local), F32),
            jnp.pad(taps, ((0, 0), (1, local - 1 - filt))),
            norm_gain.reshape(ring, local),
        ],
        axis=0,
    )
    wv = value_projection.reshape(ring, local, local)
    wo = out_projection.reshape(local, width)
    anywhere = pl.BlockSpec(memory_space=pl.ANY)
    vmem = pltpu.VMEM
    dma = pltpu.SemaphoreType.DMA
    result = pl.pallas_call(
        lambda *refs: kernel(ring, chain, rows, local, groups, min(3, half - 1), *refs),
        name="two_layers",
        out_shape=jax.ShapeDtypeStruct((rows, local), BF16),
        in_specs=[anywhere] * 4,
        out_specs=pl.BlockSpec(memory_space=pltpu.VMEM),
        scratch_shapes=[
            vmem((2, ring, rows, local), BF16),
            vmem((2, *par.shape), F32),
            vmem((2, ring, local, local), BF16),
            vmem((2, local, width), BF16),
            vmem((groups * rows, 2 * rows), BF16),
            vmem((groups * rows, local), F32),
            vmem((rows, local), F32),
            vmem((rows, 128), F32),
            vmem((2 * rows + TAIL, local), F32),
            vmem((2 * rows + TAIL, local), F32),
            vmem((2, 2, rows, local), BF16),
            vmem((2, 2, rows, local), BF16),
            vmem((2, 2, TAIL, local), BF16),
            vmem((2, rows, local), F32),
            vmem((2, 2, half, rows, local), BF16),
            vmem((2, 2, half, rows, local), BF16),
            dma,
            dma((2,)),
            dma((2,)),
            dma((2,)),
            dma((3,)),
            dma((2, 2, half, CHUNKS)),
            dma((2, 2, half, CHUNKS)),
            dma((2, 2)),
            dma((2, 2)),
            dma((2, 2, half, CHUNKS)),
            dma((2, 2, half, CHUNKS)),
        ],
        compiler_params=pltpu.CompilerParams(
            collective_id=0, has_side_effects=True, vmem_limit_bytes=60 * 1024 * 1024
        ),
    )(activations, par, wv, wo)
    return result[None]


def solution(mesh):
    in_specs = (
        P(None, "ctx", "tp"),
        P("section", None),
        P("section", None, "tp"),
        P("section", None, None, "tp"),
        P("section", "tp", None),
        P("section", "tp"),
        P("section", "tp", None),
    )
    out_specs = P("section", "ctx", "tp")
    return jax.shard_map(body, mesh=mesh, in_specs=in_specs, out_specs=out_specs, check_vma=False)
```

time: 372 us -> 149 us (0.40)
  waiting for transfers between devices: 289 us -> 0 us
  Pallas kernels: 0 us -> 140 us
  starting transfers between devices: 30.5 us -> 0 us
  matrix products: 14.4 us -> 0 us
  between operations: 13.5 us -> 0.03 us
  other arithmetic: 11.7 us -> 2.83 us
  local copies, waits for them, and re-layouts: 11.7 us -> 5.28 us
    all_gather x2 -> x0, waiting for transfers between devices: 144 us -> none  [layer(): whole = lax.all_gather(current, 'tp', axis=1, tiled=True)]
    reduce_scatter x2 -> x0, waiting for transfers between devices: 140 us -> none  [layer(): summed = lax.psum_scatter(terms, 'tp', scatter_dimension=1, tiled=True)]
    pallas_call x0 -> x1, Pallas kernels: none -> 140 us  [body(): pl.pallas_call(lambda *refs: kernel(ring, chain, rows, local, groups, min...]
    ppermute x10 -> x0, starting transfers between devices: 30.4 us -> none  [the longest x4 17.7 us: from_behind(): return lax.ppermute(shard, axis, pairs)]
    dot_general x6 -> x0, matrix products: 14.4 us -> none  [the longest x2 6.26 us: layer(): raw_proj = jnp.dot(normed, flat, preferred_element_type=jnp.float32)]
    dot_general x2 -> x0, local copies, waits for them, and re-layouts: 7.72 us -> none  [layer(): all_groups = jnp.dot(matrix, extended, preferred_element_type=jnp.float32)]
    ppermute x10 -> x0, waiting for transfers between devices: 4.95 us -> none  [the longest x4 3.58 us: from_behind(): return lax.ppermute(shard, axis, pairs)]
  transfers between devices with their start and end apart: 14 -> 0, of which waited for: 7 -> 0; matrix products, arithmetic and copies ran while one was open for 5% -> 0% of each run, Pallas kernels for 0% -> 0%
where the time goes in v1:
time: 149 us; the launch traced here: 148 us
  Pallas kernels  140 us (94%)
  local copies, waits for them, and re-layouts  5.28 us (4%)
  other arithmetic  2.83 us (2%)
    pallas_call x1, Pallas kernels, body(): pl.pallas_call(lambda *refs: kernel(ring, chain, rows, local, groups, min...  140 us
    concatenate x1, local copies, waits for them, and re-layouts, body(): jnp.concatenate([short_taps[0].reshape(9, local), skip_gain, jnp.zeros((T...  3.12 us

profile of v1, /device:TPU:6, one launch (start us, length us, event | category | flops | bytes accessed | tf_op | source)
XLA Modules:
  0.0 148.1 jit_solution(11572589929218611235)
XLA Ops:
  0.0 0.7 bitcast_convert_fusion
  0.7 0.1 rev.4
  0.8 0.1 pad.4
  0.8 0.7 reduce
  1.6 0.5 broadcast.6
  2.1 1.4 reduce.4
  3.5 3.1 %concatenate.3.refs_1_ = f32[48,256]{1,0:T(8,128)} concatenate(f32[9,256]{1,0:T(8,128)S(1)} %reshape_squeeze.3, f32[1,256]{1,0:T(1,128)} %param.12, f32[6,256]{1,0:T(8,128)S(1)} %broadcast_in_dim.6, f32[16,256]{1,0:T(8,128)S(1)} %pad.4, f32[16,256]{1,0:T(8,128)S(1)} %reshape.11), dimensions={0} | concatenate | bytes 98304 | tf_op jit(solution)/shard_map/concatenate | solution.py:260
  6.7 140.0 %two_layers.1 = bf16[128,256]{1,0:T(8,128)(2,1)} custom-call(bf16[2,128,256]{2,1,0:T(8,128)(2,1)} %refs_0_.1, f32[48,256]{1,0:T(8,128)} %concatenate.3.refs_1_, bf16[16,256,256]{2,1,0:T(8,128)(2,1)} %bitcast.6, bf16[256,4096]{1,0:T(8,128)(2,1)} %bitcast.7), custom_call_target="tpu_custom_call" | custom-call | tf_op jit(solution)/shard_map/two_layers/pallas_call | solution.py:275
  146.6 1.5 copy.10
  (3 shorter events, 0.0 us)

commit v2 on v1

v2 whole, which is shorter than its diff:
```python
import jax
import jax.numpy as jnp
from jax import lax
from jax.experimental import pallas as pl
from jax.experimental.pallas import tpu as pltpu
from jax.sharding import PartitionSpec as P

EPS = 1e-06
CHUNKS = 2
TAIL = 16
MESH = pl.DeviceIdType.MESH
F32 = jnp.float32
BF16 = jnp.bfloat16


def kernel(
    ring, chain, rows, local, groups, lag,
    act, wv_in, gain_in, taps_in, short_in, skip_in, wo_in, out,
    whole, wv, gain, taps, shorts, skips, wo,
    matrix, conv, acc, ssq, qx, vx, qv, halo, tail, term,
    far_out, far_got, near_out, near_got,
    act_sem, hold_sem, swap_sem,
    agf_s, agf_r, agn_s, agn_r, halo_s, halo_r, rsf_s, rsf_r, rsn_s, rsn_r,
):
    s = lax.axis_index("section")
    c = lax.axis_index("ctx")
    z = lax.axis_index("tp")
    half = ring // 2
    stages = half // 2
    width = ring * local
    group_width = local // groups
    part = rows // CHUNKS
    sign = (1, -1)

    def at_z(d, hops):
        return lax.rem(z + ring + sign[d] * hops, ring)

    ahead = lax.rem(c + 1, chain)
    ahead2 = lax.rem(c + 2, chain)
    behind = lax.rem(c + chain - 1, chain)
    behind2 = lax.rem(c + chain - 2, chain)

    barrier = pltpu.get_barrier_semaphore()
    for there in (
        {"section": 1 - s}, {"tp": at_z(0, 1)}, {"tp": at_z(1, 1)}, {"tp": at_z(0, 2)}, {"tp": at_z(1, 2)},
        {"ctx": ahead}, {"ctx": ahead2}, {"ctx": behind}, {"ctx": behind2},
    ):
        pl.semaphore_signal(barrier, inc=1, device_id=there, device_id_type=MESH)

    own = pltpu.make_async_copy(act.at[s], whole.at[0, z], act_sem)
    own.start()
    weights = (
        (wv_in, wv), (gain_in, gain), (taps_in, taps), (short_in, shorts), (skip_in, skips), (wo_in, wo),
    )
    for index, (source, held) in enumerate(weights):
        pltpu.make_async_copy(source, held.at[s], hold_sem.at[index, s]).start()
    pl.semaphore_wait(barrier, 9)

    def swap(index):
        source, held = weights[index]
        return pltpu.make_async_remote_copy(
            source, held.at[s], swap_sem.at[index], hold_sem.at[index, s],
            device_id={"section": 1 - s}, device_id_type=MESH,
        )

    def ready(layer, *indices):
        for index in indices:
            source, held = weights[index]
            pltpu.make_async_copy(source, held.at[layer], hold_sem.at[index, layer]).wait()

    def piece(q):
        return pl.ds(q * part, part)

    def far_in_gather(d, j):
        return 0 <= j < (stages if d == 0 else stages - 1)

    def far_in_scatter(d, i):
        return (0 if d == 0 else 1) <= i < stages

    def gather_far(layer, d, j, q, received=False):
        block = whole.at[layer, at_z(d, -2 * j - (2 if received else 0)), piece(q)]
        return pltpu.make_async_remote_copy(
            block, block, agf_s.at[layer, d, j, q], agf_r.at[layer, d, j, q],
            device_id={"tp": at_z(d, 2)}, device_id_type=MESH,
        )

    def gather_near(layer, d, j, received=False):
        block = whole.at[layer, at_z(d, -2 * j - (1 if received else 0))]
        return pltpu.make_async_remote_copy(
            block, block, agn_s.at[layer, d, j], agn_r.at[layer, d, j],
            device_id={"tp": at_z(d, 1)}, device_id_type=MESH,
        )

    def scatter_far(layer, d, i, q):
        return pltpu.make_async_remote_copy(
            far_out.at[layer, d, i, piece(q)], far_got.at[layer, d, i, piece(q)],
            rsf_s.at[layer, d, i, q], rsf_r.at[layer, d, i, q],
            device_id={"tp": at_z(d, 2)}, device_id_type=MESH,
        )

    def scatter_near(layer, d, i):
        return pltpu.make_async_remote_copy(
            near_out.at[layer, d, i], near_got.at[layer, d, i],
            rsn_s.at[layer, d, i], rsn_r.at[layer, d, i],
            device_id={"tp": at_z(d, 1)}, device_id_type=MESH,
        )

    def halo_copy(layer):
        return pltpu.make_async_remote_copy(
            qv.at[layer], halo.at[layer], halo_s.at[layer, 0], halo_r.at[layer, 0],
            device_id={"ctx": ahead}, device_id_type=MESH,
        )

    def tail_copy(layer):
        return pltpu.make_async_remote_copy(
            qv.at[layer, :, pl.ds(rows - TAIL, TAIL)], tail.at[layer],
            halo_s.at[layer, 1], halo_r.at[layer, 1],
            device_id={"ctx": ahead2}, device_id_type=MESH,
        )

    own.wait()
    for layer in range(2):
        for q in range(CHUNKS):
            for d in range(2):
                if far_in_gather(d, 0):
                    gather_far(layer, d, 0, q).start()
        for d in range(2):
            gather_near(layer, d, 0).start()
        if layer == 0:
            for index in range(6):
                swap(index).start()
        acc[...] = jnp.zeros_like(acc)
        ssq[...] = jnp.zeros_like(ssq)

        def gain_of(o, layer=layer):
            return gain[layer, :, pl.ds(pl.multiple_of(o * local, local), local)]

        def project(o, layer=layer):
            x = whole[layer, o].astype(F32)
            squared = x * x
            lanes = squared[:, :128]
            for at in range(128, local, 128):
                lanes = lanes + squared[:, at : at + 128]
            ssq[...] += lanes
            normed = (x * gain_of(o)).astype(BF16)
            acc[...] += jnp.dot(normed, wv[layer, o], preferred_element_type=F32)

        def build(g, layer=layer):
            base = jnp.broadcast_to(taps[layer, g : g + 1, :], (rows, 2 * rows))
            turned = pltpu.roll(base, 0, 1, stride=1, stride_axis=0)
            matrix[g * rows : (g + 1) * rows, :] = turned.astype(BF16)

        pending = [(z, None)]
        built = 0
        waited = False
        for j in range(stages):
            for q in range(CHUNKS):
                for d in range(2):
                    if far_in_gather(d, j):
                        gather_far(layer, d, j, q, received=True).wait_recv()
                        if far_in_gather(d, j + 1):
                            gather_far(layer, d, j + 1, q).start()
            for d in range(2):
                if far_in_gather(d, j):
                    if j + 1 < stages:
                        gather_near(layer, d, j + 1).start()
                    pending.append((at_z(d, -2 * j - 2), None))
                pending.append((at_z(d, -2 * j - 1), gather_near(layer, d, j, received=True)))
            if layer == 0 and j < lag:
                continue
            if not waited:
                ready(layer, 0, 1, 2)
                waited = True
            count = 8 if j + 1 < stages else len(pending)
            for o, copy in pending[:count]:
                if copy is not None:
                    copy.wait_recv()
                project(o)
            pending = pending[count:]
            goal = groups * (j + 1) // stages
            for g in range(built, goal):
                build(g)
            built = goal

        def short(i, which, layer=layer):
            return shorts[layer, i, which : which + 1, :]

        def featured(which, x, start, count):
            return (
                short(0, which) * x[start : start + count, :]
                + short(1, which) * x[start - 1 : start - 1 + count, :]
                + short(2, which) * x[start - 2 : start - 2 + count, :]
            )

        scale = lax.rsqrt(jnp.sum(ssq[...], axis=1, keepdims=True) / width + EPS)
        values = (acc[...] * scale).astype(BF16)
        normed = (whole[layer, z].astype(F32) * gain_of(z)).astype(BF16)
        query = (normed.astype(F32) * scale).astype(BF16)
        qv[layer, 1] = values
        qv[layer, 0] = query
        halo_copy(layer).start()
        tail_copy(layer).start()
        qx[TAIL + rows :, :] = query.astype(F32)
        vx[TAIL + rows :, :] = values.astype(F32)
        ready(layer, 3, 4)
        halo_copy(layer).wait_recv()
        tail_copy(layer).wait_recv()
        for index, x in ((0, qx), (1, vx)):
            x[TAIL : TAIL + rows, :] = jnp.where(c > 0, halo[layer, index].astype(F32), 0.0)
            x[:TAIL, :] = jnp.where(c > 1, tail[layer, index].astype(F32), 0.0)
        product = (
            featured(1, qx, TAIL, 2 * rows) * featured(2, vx, TAIL, 2 * rows)
        ).astype(BF16)
        conv[...] = jnp.dot(matrix[...], product, preferred_element_type=F32)
        group_of = lax.broadcasted_iota(jnp.int32, (rows, local), 1) // group_width
        filtered = conv[:rows, :]
        for g in range(1, groups):
            filtered = jnp.where(group_of == g, conv[g * rows : (g + 1) * rows, :], filtered)
        mixed = filtered + skips[layer] * product[rows:, :].astype(F32)
        gated = (featured(0, qx, TAIL + rows, rows) * mixed).astype(BF16)
        ready(layer, 5)

        def terms(dest, layer=layer, gated=gated):
            columns = pl.ds(pl.multiple_of(dest * local, local), local)
            return jnp.dot(gated, wo[layer, :, columns], preferred_element_type=F32)

        def send_near(i, layer=layer):
            for d in range(2):
                near_out[layer, d, i] = terms(at_z(d, half - 2 * i - 1)).astype(BF16)
                scatter_near(layer, d, i).start()

        far_out[layer, 0, 0] = terms(at_z(0, half)).astype(BF16)
        for q in range(CHUNKS):
            scatter_far(layer, 0, 0, q).start()
        send_near(0)
        for i in range(1, stages):
            for d in range(2):
                term[d] = terms(at_z(d, half - 2 * i))
            send_near(i)
            for d in (1, 0):
                scatter_near(layer, d, i - 1).wait_recv()
            for q in range(CHUNKS):
                for d in (1, 0):
                    total = term[d, piece(q)] + near_got[layer, d, i - 1, piece(q)].astype(F32)
                    if far_in_scatter(d, i - 1):
                        scatter_far(layer, d, i - 1, q).wait_recv()
                        total = total + far_got[layer, d, i - 1, piece(q)].astype(F32)
                    far_out[layer, d, i, piece(q)] = total.astype(BF16)
                    scatter_far(layer, d, i, q).start()
        term[0] = whole[layer, z].astype(F32)
        term[1] = terms(z)
        for d in range(2):
            scatter_near(layer, d, stages - 1).wait_recv()
        for q in range(CHUNKS):
            summed = term[1, piece(q)]
            for d in range(2):
                summed = summed + near_got[layer, d, stages - 1, piece(q)].astype(F32)
                if far_in_scatter(d, stages - 1):
                    scatter_far(layer, d, stages - 1, q).wait_recv()
                    summed = summed + far_got[layer, d, stages - 1, piece(q)].astype(F32)
            result = (term[0, piece(q)] + summed).astype(BF16)
            if layer == 0:
                whole[1, z, piece(q)] = result
            else:
                out[piece(q), :] = result

    for index in range(6):
        swap(index).wait_send()
    for layer in range(2):
        halo_copy(layer).wait_send()
        tail_copy(layer).wait_send()
        for d in range(2):
            for j in range(stages):
                gather_near(layer, d, j).wait_send()
                scatter_near(layer, d, j).wait_send()
                for q in range(CHUNKS):
                    if far_in_gather(d, j):
                        gather_far(layer, d, j, q).wait_send()
                    if far_in_scatter(d, j):
                        scatter_far(layer, d, j, q).wait_send()


def body(
    activations, norm_gain, value_projection, short_taps, long_taps, skip_gain, out_projection
):
    ring = lax.axis_size("tp")
    chain = lax.axis_size("ctx")
    rows, local = activations.shape[1:]
    width = value_projection.shape[1]
    groups, filt = long_taps.shape[1:]
    stages = ring // 4
    turned = jnp.flip(long_taps[0].astype(F32), axis=1)
    taps = jnp.pad(turned, ((0, 0), (1, local - 1 - filt)))
    wv = value_projection.reshape(ring, local, local)
    wo = out_projection.reshape(local, width)
    anywhere = pl.BlockSpec(memory_space=pl.ANY)
    vmem = pltpu.VMEM
    dma = pltpu.SemaphoreType.DMA
    result = pl.pallas_call(
        lambda *refs: kernel(ring, chain, rows, local, groups, min(1, stages - 1), *refs),
        name="two_layers",
        out_shape=jax.ShapeDtypeStruct((rows, local), BF16),
        in_specs=[anywhere] * 7,
        out_specs=pl.BlockSpec(memory_space=pltpu.VMEM),
        scratch_shapes=[
            vmem((2, ring, rows, local), BF16),
            vmem((2, ring, local, local), BF16),
            vmem((2, 1, width), F32),
            vmem((2, *taps.shape), F32),
            vmem((2, 3, 3, local), F32),
            vmem((2, 1, local), F32),
            vmem((2, local, width), BF16),
            vmem((groups * rows, 2 * rows), BF16),
            vmem((groups * rows, local), F32),
            vmem((rows, local), F32),
            vmem((rows, 128), F32),
            vmem((2 * rows + TAIL, local), F32),
            vmem((2 * rows + TAIL, local), F32),
            vmem((2, 2, rows, local), BF16),
            vmem((2, 2, rows, local), BF16),
            vmem((2, 2, TAIL, local), BF16),
            vmem((2, rows, local), F32),
            vmem((2, 2, stages, rows, local), BF16),
            vmem((2, 2, stages, rows, local), BF16),
            vmem((2, 2, stages, rows, local), BF16),
            vmem((2, 2, stages, rows, local), BF16),
            dma,
            dma((6, 2)),
            dma((6,)),
            dma((2, 2, stages, CHUNKS)),
            dma((2, 2, stages, CHUNKS)),
            dma((2, 2, stages)),
            dma((2, 2, stages)),
            dma((2, 2)),
            dma((2, 2)),
            dma((2, 2, stages, CHUNKS)),
            dma((2, 2, stages, CHUNKS)),
            dma((2, 2, stages)),
            dma((2, 2, stages)),
        ],
        compiler_params=pltpu.CompilerParams(
            collective_id=0, has_side_effects=True, vmem_limit_bytes=60 * 1024 * 1024
        ),
    )(activations, wv, norm_gain, taps, short_taps[0], skip_gain, wo)
    return result[None]


def solution(mesh):
    in_specs = (
        P(None, "ctx", "tp"),
        P("section", None),
        P("section", None, "tp"),
        P("section", None, None, "tp"),
        P("section", "tp", None),
        P("section", "tp"),
        P("section", "tp", None),
    )
    out_specs = P("section", "ctx", "tp")
    return jax.shard_map(body, mesh=mesh, in_specs=in_specs, out_specs=out_specs, check_vma=False)
```

time: 149 us -> 117 us (0.79)
  Pallas kernels: 140 us -> 112 us
  other arithmetic: 2.83 us -> 0.69 us
  local copies, waits for them, and re-layouts: 5.28 us -> 3.53 us
    pallas_call x1, Pallas kernels: 140 us -> 112 us  [body(): pl.pallas_call(lambda *refs: kernel(ring, chain, rows, local, groups, min...]
    concatenate x1 -> x0, local copies, waits for them, and re-layouts: 3.12 us -> none  [body(): jnp.concatenate([short_taps[0].reshape(9, local), skip_gain, jnp.zeros((T...]
    unnamed x2 -> x0, other arithmetic: 2.14 us -> none
where the time goes in v2:
time: 117 us; the launch traced here: 116 us
  Pallas kernels  112 us (96%)
  local copies, waits for them, and re-layouts  3.53 us (3%)
    pallas_call x1, Pallas kernels, body(): pl.pallas_call(lambda *refs: kernel(ring, chain, rows, local, groups, min...  112 us
    unnamed x2, local copies, waits for them, and re-layouts  2.77 us

profile of v2, /device:TPU:6, one launch (start us, length us, event | category | flops | bytes accessed | tf_op | source)
XLA Modules:
  0.0 115.7 jit_solution(16229663734442370931)
XLA Ops:
  0.0 0.7 bitcast_convert_fusion
  0.7 0.1 rev.4
  0.8 0.7 pad.4.refs_3_
  1.4 1.3 %copy.10 = f32[1,3,3,256]{3,2,0,1:T(4,128)} copy(f32[1,3,3,256]{3,0,2,1:T(1,128)} %param.10) | data formatting | bytes 18432
  2.7 111.5 %two_layers.1 = bf16[128,256]{1,0:T(8,128)(2,1)} custom-call(bf16[2,128,256]{2,1,0:T(8,128)(2,1)} %refs_0_.1, bf16[16,256,256]{2,1,0:T(8,128)(2,1)} %bitcast.9, f32[1,4096]{1,0:T(1,128)} %refs_2_.1, f32[16,256]{1,0:T(8,128)} %pad.4.refs_3_, f32[3,3,256]{2,1,0:T(4,128)} %bitcast.12, f32[1,256]{1,0:T(1,128)} %refs_5_.1, bf16[256,4096]{1,0:T(8,128)(2,1)} %bitcast.10), custom_call_target="tpu_custom_call" | custom-call | tf_op jit(solution)/shard_map/two_layers/pallas_call | solution.py:299
  114.3 1.5 %copy.12 = bf16[1,128,256]{2,1,0:T(8,128)(2,1)} copy(bf16[1,128,256]{2,1,0:T(8,128)(2,1)} %bitcast.11) | data formatting | bytes 131072

commit v3 on v2

--- a/solution.py
+++ b/solution.py
@@ -6,7 +6,7 @@
 from jax.sharding import PartitionSpec as P
 
 EPS = 1e-06
-CHUNKS = 2
+CHUNKS = 4
 TAIL = 16
 MESH = pl.DeviceIdType.MESH
 F32 = jnp.float32
@@ -17,7 +17,7 @@
     ring, chain, rows, local, groups, lag,
     act, wv_in, gain_in, taps_in, short_in, skip_in, wo_in, out,
     whole, wv, gain, taps, shorts, skips, wo,
-    matrix, conv, acc, ssq, qx, vx, qv, halo, tail, term,
+    matrix, conv, acc, ssq, qx, vx, qv, halo, tail, scale_out, scale_got, term,
     far_out, far_got, near_out, near_got,
     act_sem, hold_sem, swap_sem,
     agf_s, agf_r, agn_s, agn_r, halo_s, halo_r, rsf_s, rsf_r, rsn_s, rsn_r,
@@ -105,11 +105,20 @@
             device_id={"tp": at_z(d, 1)}, device_id_type=MESH,
         )
 
+    def to_next(source, target, layer, index):
+        return pltpu.make_async_remote_copy(
+            source, target, halo_s.at[layer, index], halo_r.at[layer, index],
+            device_id={"ctx": ahead}, device_id_type=MESH,
+        )
+
+    def block_copy(layer):
+        return to_next(whole.at[layer, z], halo.at[layer, 0], layer, 0)
+
     def halo_copy(layer):
-        return pltpu.make_async_remote_copy(
-            qv.at[layer], halo.at[layer], halo_s.at[layer, 0], halo_r.at[layer, 0],
-            device_id={"ctx": ahead}, device_id_type=MESH,
-        )
+        return to_next(qv.at[layer, 1], halo.at[layer, 1], layer, 2)
+
+    def scale_copy(layer):
+        return to_next(scale_out.at[layer], scale_got.at[layer], layer, 3)
 
     def tail_copy(layer):
         return pltpu.make_async_remote_copy(
@@ -126,6 +135,7 @@
                     gather_far(layer, d, 0, q).start()
         for d in range(2):
             gather_near(layer, d, 0).start()
+        block_copy(layer).start()
         if layer == 0:
             for index in range(6):
                 swap(index).start()
@@ -194,19 +204,33 @@
 
         scale = lax.rsqrt(jnp.sum(ssq[...], axis=1, keepdims=True) / width + EPS)
         values = (acc[...] * scale).astype(BF16)
-        normed = (whole[layer, z].astype(F32) * gain_of(z)).astype(BF16)
-        query = (normed.astype(F32) * scale).astype(BF16)
         qv[layer, 1] = values
+        halo_copy(layer).start()
+        eye = lax.broadcasted_iota(jnp.int32, (rows, rows), 0) == lax.broadcasted_iota(
+            jnp.int32, (rows, rows), 1
+        )
+        scale_row = jnp.sum(jnp.where(eye, scale, 0.0), axis=0, keepdims=True)
+        scale_out[layer] = jnp.broadcast_to(scale_row, (8, rows))
+        scale_copy(layer).start()
+
+        def query_of(block, by):
+            normed = (block.astype(F32) * gain_of(z)).astype(BF16)
+            return (normed.astype(F32) * by).astype(BF16)
+
+        query = query_of(whole[layer, z], scale)
         qv[layer, 0] = query
-        halo_copy(layer).start()
         tail_copy(layer).start()
         qx[TAIL + rows :, :] = query.astype(F32)
         vx[TAIL + rows :, :] = values.astype(F32)
         ready(layer, 3, 4)
+        block_copy(layer).wait_recv()
+        scale_copy(layer).wait_recv()
+        scale_behind = jnp.sum(jnp.where(eye, scale_got[layer, :1, :], 0.0), axis=1, keepdims=True)
+        query_behind = query_of(halo[layer, 0], scale_behind)
         halo_copy(layer).wait_recv()
         tail_copy(layer).wait_recv()
-        for index, x in ((0, qx), (1, vx)):
-            x[TAIL : TAIL + rows, :] = jnp.where(c > 0, halo[layer, index].astype(F32), 0.0)
+        for index, x, block in ((0, qx, query_behind), (1, vx, halo[layer, 1])):
+            x[TAIL : TAIL + rows, :] = jnp.where(c > 0, block.astype(F32), 0.0)
             x[:TAIL, :] = jnp.where(c > 1, tail[layer, index].astype(F32), 0.0)
         product = (
             featured(1, qx, TAIL, 2 * rows) * featured(2, vx, TAIL, 2 * rows)
@@ -267,7 +291,9 @@
     for index in range(6):
         swap(index).wait_send()
     for layer in range(2):
+        block_copy(layer).wait_send()
         halo_copy(layer).wait_send()
+        scale_copy(layer).wait_send()
         tail_copy(layer).wait_send()
         for d in range(2):
             for j in range(stages):
@@ -319,6 +345,8 @@
             vmem((2, 2, rows, local), BF16),
             vmem((2, 2, rows, local), BF16),
             vmem((2, 2, TAIL, local), BF16),
+            vmem((2, 8, rows), F32),
+            vmem((2, 8, rows), F32),
             vmem((2, rows, local), F32),
             vmem((2, 2, stages, rows, local), BF16),
             vmem((2, 2, stages, rows, local), BF16),
@@ -331,8 +359,8 @@
             dma((2, 2, stages, CHUNKS)),
             dma((2, 2, stages)),
             dma((2, 2, stages)),
-            dma((2, 2)),
-            dma((2, 2)),
+            dma((2, 4)),
+            dma((2, 4)),
             dma((2, 2, stages, CHUNKS)),
             dma((2, 2, stages, CHUNKS)),
             dma((2, 2, stages)),

time: 117 us -> 116 us (level)
  Pallas kernels: 112 us -> 110 us
    pallas_call x1, Pallas kernels: 112 us -> 110 us  [body(): pl.pallas_call(lambda *refs: kernel(ring, chain, rows, local, groups, min...]
where the time goes in v3:
time: 116 us; the launch traced here: 114 us
  Pallas kernels  110 us (95%)
  local copies, waits for them, and re-layouts  3.53 us (3%)
    pallas_call x1, Pallas kernels, body(): pl.pallas_call(lambda *refs: kernel(ring, chain, rows, local, groups, min...  110 us
    unnamed x2, local copies, waits for them, and re-layouts  2.77 us

profile of v3, /device:TPU:6, one launch (start us, length us, event | category | flops | bytes accessed | tf_op | source)
XLA Modules:
  0.0 114.2 jit_solution(2558071473935421666)
XLA Ops:
  0.0 0.7 bitcast_convert_fusion
  0.7 0.1 rev.4
  0.8 0.7 pad.4.refs_3_
  1.4 1.3 %copy.10 = f32[1,3,3,256]{3,2,0,1:T(4,128)} copy(f32[1,3,3,256]{3,0,2,1:T(1,128)} %param.10) | data formatting | bytes 18432
  2.7 110.0 %two_layers.1 = bf16[128,256]{1,0:T(8,128)(2,1)} custom-call(bf16[2,128,256]{2,1,0:T(8,128)(2,1)} %refs_0_.1, bf16[16,256,256]{2,1,0:T(8,128)(2,1)} %bitcast.9, f32[1,4096]{1,0:T(1,128)} %refs_2_.1, f32[16,256]{1,0:T(8,128)} %pad.4.refs_3_, f32[3,3,256]{2,1,0:T(4,128)} %bitcast.12, f32[1,256]{1,0:T(1,128)} %refs_5_.1, bf16[256,4096]{1,0:T(8,128)(2,1)} %bitcast.10), custom_call_target="tpu_custom_call" | custom-call | tf_op jit(solution)/shard_map/two_layers/pallas_call | solution.py:325
  112.7 1.5 %copy.12 = bf16[1,128,256]{2,1,0:T(8,128)(2,1)} copy(bf16[1,128,256]{2,1,0:T(8,128)(2,1)} %bitcast.11) | data formatting | bytes 131072
